TPU v7x, 32 devices: a whole 2x2x4 slice. The times are simulated.
32 devices in a mesh: freq: 2 (over y), row: 4 (over z), col: 4 (over x, core).
Axes of the slice: x: 2, y: 2, z: 4, core: 2. Of those that a mesh axis runs over, the one named last changes fastest.
Arguments:
- traces: bfloat16 [4, 6144, 6144], P('freq', 'row', 'col'), parts along dimension 0, may hold values from -6 to 6
- recv_live: int32 [12288], P('freq'), parts along dimension 0, may hold values 0 or 1
- missing: int32 [8, 96], P('freq'), parts along dimension 0, may hold values from 0 to 1535, as said below
- wavelet: float32 [4], P('freq'), parts along dimension 0, may hold values from 0.5 to 1.5
Outputs:
- primaries: float32 [4, 6144, 512], P('freq', 'row', 'col'), parts along dimension 0
There are 2 independent parts, one for each index of `freq`. A program takes and returns all parts, laid end to end along the dimension named above; each array names one. Nothing has to cross between parts.
Inputs may be any that keep to these rules, and one draw needn't show every extreme that they name: `missing`: each row lists 96 distinct positions within one block of 1536 shots, the shots of that block that were not recorded; the block's first and last shots are always among them.
All inputs are finite; a program needn't handle non-finite values.
Results may differ from a plain program's by a relative error of at most 0.0003.
Values may be sent and summed in bfloat16 or wider, within the bound.
A program may use at most 128 MiB of HBM per device.

v0:
```python
import math
import jax
import jax.numpy as jnp
from jax import lax
from jax.sharding import PartitionSpec as P

ORDER = 6144
WIN = 128


def from_behind(block, axis, distance):
    devices = range(lax.axis_size(axis))
    route = [((i - distance) % len(devices), i) for i in devices]
    return lax.ppermute(block, axis, route)


def matmul(first, second):
    return jnp.dot(first, second, preferred_element_type=jnp.float32)


def complex_product(left_tile, right_tile):
    real_part = matmul(left_tile[0], right_tile[0]) - matmul(left_tile[1], right_tile[1])
    imag_part = matmul(left_tile[0], right_tile[1]) + matmul(left_tile[1], right_tile[0])
    return jnp.stack([real_part, imag_part])


def mirror(payload, grid_size, row_index, col_index):
    anti_sum = row_index + col_index
    anchors = jnp.arange(grid_size, dtype=jnp.int32)
    bit_count = grid_size.bit_length() - 1
    for bit_number in range(bit_count):
        stride = 2**bit_number
        carried = from_behind(payload, "row", stride)
        carried = from_behind(carried, "col", grid_size - stride)
        offset = (anti_sum - 2 * anchors) % grid_size
        spot_row = (anchors + offset % stride) % grid_size
        arrive = jnp.any(
            (spot_row == (row_index - stride) % grid_size) & (offset // stride % 2 == 1)
        )
        payload = jnp.where(arrive, carried, payload)
    return payload


def transpose_blocks(payload, grid_size, row_index, col_index):
    anti_sum = row_index + col_index
    anchors = jnp.arange(grid_size, dtype=jnp.int32)
    bit_count = grid_size.bit_length() - 1
    for bit_number in range(bit_count):
        stride = 2**bit_number
        carried = from_behind(payload, "row", stride)
        carried = from_behind(carried, "col", grid_size - stride)
        offset = (anti_sum - 2 * anchors) % grid_size
        spot_row = (anchors + offset % stride) % grid_size
        arrive = jnp.any(
            (spot_row == (row_index - stride) % grid_size) & (offset // stride % 2 == 1)
        )
        payload = jnp.where(arrive, carried, payload)
    return payload


def local(traces, recv_live, missing, wavelet):
    tile_size = traces.shape[1]
    grid_size = lax.axis_size("row")
    row_index = lax.axis_index("row")
    col_index = lax.axis_index("col")
    positions = jnp.arange(tile_size, dtype=jnp.int32)
    miss_row = lax.dynamic_index_in_dim(missing, row_index, 0, keepdims=False)
    miss_col = lax.dynamic_index_in_dim(missing, col_index, 0, keepdims=False)
    dead_row = jnp.any(positions[:, None] == miss_row[None, :], axis=1)
    dead_col = jnp.any(positions[:, None] == miss_col[None, :], axis=1)
    recv_row = lax.dynamic_slice_in_dim(recv_live, row_index * tile_size, tile_size) == 1
    recv_col = lax.dynamic_slice_in_dim(recv_live, col_index * tile_size, tile_size) == 1
    zero_bf = jnp.zeros((), jnp.bfloat16)
    outgoing = jnp.swapaxes(jnp.take(traces, miss_col, axis=2), 1, 2)
    incoming = mirror(outgoing, grid_size, row_index, col_index)
    direct = jnp.where(recv_col[None, None, :], traces, zero_bf)
    direct = jnp.where(dead_row[None, :, None], zero_bf, direct)
    keep_mask = jnp.take(recv_row, miss_row)[:, None] & jnp.logical_not(dead_col)[None, :]
    patched = jnp.where(keep_mask[None], incoming, zero_bf)
    filled = direct.at[:, miss_row, :].set(patched)
    window = filled[:, :, :WIN]
    win_width = window.shape[2]
    running = jnp.zeros((2, tile_size, win_width), jnp.float32)
    swapped = transpose_blocks(window, grid_size, row_index, col_index)
    gathered = lax.all_gather(swapped, "row", axis=2, tiled=True)

    def one_hop(stop_index, total):
        source_block = (col_index - stop_index - 1) % grid_size
        piece = lax.dynamic_slice_in_dim(gathered, source_block * win_width, win_width, 2)
        total = total + complex_product(filled, piece)
        return from_behind(total, "col", 1)

    running = lax.fori_loop(0, grid_size - 1, one_hop, running)
    own_piece = lax.dynamic_slice_in_dim(gathered, col_index * win_width, win_width, 2)
    running = running + complex_product(filled, own_piece)
    norm_scale = 1.0 / math.sqrt(ORDER)
    pred_real = (wavelet[0] * running[0] - wavelet[1] * running[1]) * norm_scale
    pred_imag = (wavelet[0] * running[1] + wavelet[1] * running[0]) * norm_scale
    window_f = window.astype(jnp.float32)
    return jnp.stack([window_f[0] - pred_real, window_f[1] - pred_imag])


def solution(mesh):
    in_specs = (P("freq", "row", "col"), P("freq"), P("freq", None), P("freq"))
    out_specs = P("freq", "row", "col")
    return jax.shard_map(local, mesh=mesh, in_specs=in_specs, out_specs=out_specs, check_vma=False)
```

profile of v0, /device:TPU:0, one launch (start us, length us, event | category | flops | bytes accessed | tf_op | source)
XLA Modules:
  0.0 447.0 jit_solution(11039672735321170451)
XLA Ops:
  10.2 24.0 %copy.16 = bf16[2,1536,1536]{1,0,2:T(2,128)(2,1)} copy(bf16[2,1536,1536]{2,1,0:T(8,128)(2,1)} %param.6) | data formatting | bytes 18874368 | tf_op args[0]
  34.2 5.5 %gather_fusion.1 = bf16[96,2,1536]{2,1,0:T(2,128)(2,1)S(1)} fusion(bf16[2,1536,1536]{1,0,2:T(2,128)(2,1)} %copy.16, s32[1024]{0:T(1024)S(1)} %get-tuple-element.183), kind=kCustom, calls=%fused_computation.1 | custom fusion | bytes 1180032 | tf_op jit(solution)/shard_map/jit(_take)/gather | solution.py:74
  43.4 15.3 %collective-permute-done.1 = bf16[2,96,1536]{2,0,1:T(2,128)(2,1)S(1)} collective-permute-done((bf16[2,96,1536]{2,0,1:T(2,128)(2,1)S(1)}, bf16[2,96,1536]{2,0,1:T(2,128)(2,1)S(1)}, u32[]{:S(2)}, u32[]{:S(2)}) %collective-permute-start.1) | collective-permute-done | bytes 589856 | tf_op jit(solution)/shard_map/ppermute | solution.py:14
  59.6 6.7 %collective-permute-done.2 = bf16[2,96,1536]{2,0,1:T(2,128)(2,1)S(1)} collective-permute-done((bf16[2,96,1536]{2,0,1:T(2,128)(2,1)S(1)}, bf16[2,96,1536]{2,0,1:T(2,128)(2,1)S(1)}, u32[]{:S(2)}, u32[]{:S(2)}) %collective-permute-start.2) | collective-permute-done | bytes 589856 | tf_op jit(solution)/shard_map/ppermute | solution.py:14
  68.7 27.9 %collective-permute-done.3 = bf16[2,96,1536]{2,0,1:T(2,128)(2,1)S(1)} collective-permute-done((bf16[2,96,1536]{2,0,1:T(2,128)(2,1)S(1)}, bf16[2,96,1536]{2,0,1:T(2,128)(2,1)S(1)}, u32[]{:S(2)}, u32[]{:S(2)}) %collective-permute-start.3) | collective-permute-done | bytes 589856 | tf_op jit(solution)/shard_map/ppermute | solution.py:14
  98.0 42.0 %broadcast_select_fusion = bf16[2,1536,1536]{2,0,1:T(2,128)(2,1)} fusion(pred[1536]{0:T(1024)(128)(4,1)S(1)} %fusion.54, pred[1536]{0:T(1024)(128)(4,1)S(1)} %get-tuple-element.175, bf16[2,1536,1536]{2,1,0:T(8,128)(2,1)} %param.6), kind=kLoop, calls=%fused_computation.26 | loop fusion | flops 9437184 | bytes 18877440 | tf_op jit(solution)/shard_map/jit(_where)/select_n | solution.py:77
  142.6 11.7 %scatter_fusion = bf16[2,1536,1536]{2,0,1:T(2,128)(2,1)} fusion(bf16[2,1536,1536]{2,0,1:T(2,128)(2,1)} %broadcast_select_fusion, s32[96]{0:T(128)S(1)} %get-tuple-element.178, bf16[96,2,1536]{2,1,0:T(2,128)(2,1)S(1)} %fusion.52), kind=kCustom, calls=%fused_computation.2 | custom fusion | bytes 1769856 | tf_op jit(solution)/shard_map/scatter | solution.py:80
  154.3 8.8 %copy.17 = bf16[2,1536,1536]{2,1,0:T(8,128)(2,1)} copy(bf16[2,1536,1536]{2,0,1:T(2,128)(2,1)} %scatter_fusion) | data formatting | bytes 18874368 | tf_op jit(solution)/shard_map/scatter | solution.py:80
  164.4 21.1 %collective-permute-done.5 = bf16[2,1536,128]{2,1,0:T(8,128)(2,1)S(1)} collective-permute-done((bf16[2,1536,128]{2,1,0:T(8,128)(2,1)S(1)}, bf16[2,1536,128]{2,1,0:T(8,128)(2,1)S(1)}, u32[]{:S(2)}, u32[]{:S(2)}) %collective-permute-start.5) | collective-permute-done | bytes 786464 | tf_op jit(solution)/shard_map/ppermute | solution.py:14
  185.4 9.5 %collective-permute-done.6 = bf16[2,1536,128]{2,1,0:T(8,128)(2,1)S(1)} collective-permute-done((bf16[2,1536,128]{2,1,0:T(8,128)(2,1)S(1)}, bf16[2,1536,128]{2,1,0:T(8,128)(2,1)S(1)}, u32[]{:S(2)}, u32[]{:S(2)}) %collective-permute-start.6) | collective-permute-done | bytes 786464 | tf_op jit(solution)/shard_map/ppermute | solution.py:14
  198.0 36.1 %collective-permute-done.7 = bf16[2,1536,128]{2,1,0:T(8,128)(2,1)S(1)} collective-permute-done((bf16[2,1536,128]{2,1,0:T(8,128)(2,1)S(1)}, bf16[2,1536,128]{2,1,0:T(8,128)(2,1)S(1)}, u32[]{:S(2)}, u32[]{:S(2)}) %collective-permute-start.7) | collective-permute-done | bytes 786464 | tf_op jit(solution)/shard_map/ppermute | solution.py:14
  234.9 18.7 %collective-permute-done.8 = bf16[2,1536,128]{2,1,0:T(8,128)(2,1)S(1)} collective-permute-done((bf16[2,1536,128]{2,1,0:T(8,128)(2,1)S(1)}, bf16[2,1536,128]{2,1,0:T(8,128)(2,1)S(1)}, u32[]{:S(2)}, u32[]{:S(2)}) %collective-permute-start.8) | collective-permute-done | bytes 786464 | tf_op jit(solution)/shard_map/ppermute | solution.py:14
  255.8 19.5 %fusion.69 = (bf16[1,1536,1536]{2,0,1:T(2,128)(2,1)}, bf16[1,1536,1536]{2,0,1:T(2,128)(2,1)}) fusion(bf16[2,1536,1536]{2,0,1:T(2,128)(2,1)} %scatter_fusion), kind=kLoop, calls=%fused_computation.104 | loop fusion | bytes 18874368 | tf_op jit(solution)/shard_map/slice | solution.py:22
  275.4 42.8 %all-gather.2.cloned.1.call-done = bf16[2,1536,512]{2,1,0:T(8,128)(2,1)} async-done(((bf16[2,1536,128]{2,1,0:T(8,128)(2,1)}), bf16[2,1536,512]{2,1,0:T(8,128)(2,1)}) %all-gather.2.cloned.1.call-update) | async-done | bytes 3145744 | tf_op jit(solution)/shard_map/all_gather | solution.py:85
  318.3 101.8 %while.15 = (s32[]{:T(128)}, f32[2,1536,128]{1,2,0:T(8,128)S(1)}, s32[]{:T(128)}, bf16[2,1536,512]{2,1,0:T(8,128)(2,1)}, bf16[2,1536,1536]{2,1,0:T(8,128)(2,1)},...) while((s32[]{:T(128)}, f32[2,1536,128]{1,2,0:T(8,128)S(1)}, ...), condition=%wide.region_6.7_spmd, body=%wide.region_5.6_spmd.sunk | while | flops 2417098752 | bytes 73925016 | solution.py:93
  318.4 4.3 fusion.83
  322.7 4.2 fusion.85
  332.5 19.8 %collective-permute-done = f32[2,1536,128]{1,2,0:T(8,128)S(1)} collective-permute-done((f32[2,1536,128]{1,2,0:T(8,128)S(1)}, f32[2,1536,128]{1,2,0:T(8,128)S(1)}, u32[]{:S(2)}, u32[]{:S(2)}) %collective-permute-start) | collective-permute-done | bytes 1572896 | tf_op jit(solution)/shard_map/while/body/eval_jaxpr/ppermute | solution.py:14
  352.3 4.3 fusion.83
  366.4 19.8 %collective-permute-done = f32[2,1536,128]{1,2,0:T(8,128)S(1)} collective-permute-done((f32[2,1536,128]{1,2,0:T(8,128)S(1)}, f32[2,1536,128]{1,2,0:T(8,128)S(1)}, u32[]{:S(2)}, u32[]{:S(2)}) %collective-permute-start) | collective-permute-done | bytes 1572896 | tf_op jit(solution)/shard_map/while/body/eval_jaxpr/ppermute | solution.py:14
  386.2 4.3 fusion.83
  400.3 19.8 %collective-permute-done = f32[2,1536,128]{1,2,0:T(8,128)S(1)} collective-permute-done((f32[2,1536,128]{1,2,0:T(8,128)S(1)}, f32[2,1536,128]{1,2,0:T(8,128)S(1)}, u32[]{:S(2)}, u32[]{:S(2)}) %collective-permute-start) | collective-permute-done | bytes 1572896 | tf_op jit(solution)/shard_map/while/body/eval_jaxpr/ppermute | solution.py:14
  420.6 5.3 %fusion.28 = f32[1536,128]{1,0:T(8,128)S(1)} fusion(bf16[1,1536,1536]{2,0,1:T(2,128)(2,1)} %get-tuple-element.170, bf16[2,1536,512]{2,1,0:T(8,128)(2,1)} %get-tuple-element.269, s32[]{:T(128)S(6)} %select_n.231), kind=kOutput, calls=%fused_computation.28 | convolution fusion | flops 603979776 | bytes 10616836 | tf_op jit(solution)/shard_map/dot_general | solution.py:18
  425.9 5.2 %fusion.30 = f32[1536,128]{1,0:T(8,128)S(1)} fusion(bf16[1,1536,1536]{2,0,1:T(2,128)(2,1)} %get-tuple-element.170, bf16[2,1536,512]{2,1,0:T(8,128)(2,1)} %get-tuple-element.269, s32[]{:T(128)S(6)} %add.229, s32[]{:T(128)S(6)} %select_n.231), kind=kOutput, calls=%fused_computation.30 | convolution fusion | flops 603979776 | bytes 10616840 | tf_op jit(solution)/shard_map/dot_general | solution.py:18
  (67 shorter events, 56.7 us)
Async XLA Ops:
  6.5 311.6 %all-gather.2.cloned.1.call-start = ((), (), s32[]{:S(2)}) async-start(), calls=%async_computation | async-start | bytes 3932160 | tf_op jit(solution)/shard_map/all_gather | solution.py:85
  40.3 18.4 %collective-permute-start.1 = (bf16[2,96,1536]{2,0,1:T(2,128)(2,1)S(1)}, bf16[2,96,1536]{2,0,1:T(2,128)(2,1)S(1)}, u32[]{:S(2)}, u32[]{:S(2)}) collective-permute-start(bf16[2,96,1536]{2,0,1:T(2,128)(2,1)S(1)} %fusion.53), channel_id=1, source_target_pairs={{12,0},{0,4},{4,8},{8,12},{13,1},{1,5},{5,9},{9,13},{14,2},{2,6},{... | collective-permute-start | bytes 1769480 | tf_op jit(solution)/shard_map/ppermute | solution.py:14
  58.7 7.6 %collective-permute-start.2 = (bf16[2,96,1536]{2,0,1:T(2,128)(2,1)S(1)}, bf16[2,96,1536]{2,0,1:T(2,128)(2,1)S(1)}, u32[]{:S(2)}, u32[]{:S(2)}) collective-permute-start(bf16[2,96,1536]{2,0,1:T(2,128)(2,1)S(1)} %collective-permute-done.1), channel_id=1, source_target_pairs={{1,0},{2,1},{3,2},{0,3},{5,4},{6,5},{7,6},{4,7},{9,8},{10,9},{11,1... | collective-permute-start | bytes 1769480 | tf_op jit(solution)/shard_map/ppermute | solution.py:14
  67.8 28.7 %collective-permute-start.3 = (bf16[2,96,1536]{2,0,1:T(2,128)(2,1)S(1)}, bf16[2,96,1536]{2,0,1:T(2,128)(2,1)S(1)}, u32[]{:S(2)}, u32[]{:S(2)}) collective-permute-start(bf16[2,96,1536]{2,0,1:T(2,128)(2,1)S(1)} %broadcast_select_fusion.3), channel_id=1, source_target_pairs={{8,0},{12,4},{0,8},{4,12},{9,1},{13,5},{1,9},{5,13},{10,2},{14,6},... | collective-permute-start | bytes 1769480 | tf_op jit(solution)/shard_map/ppermute | solution.py:14
  96.6 44.3 %collective-permute-start.4 = (bf16[2,96,1536]{2,0,1:T(2,128)(2,1)S(1)}, bf16[2,96,1536]{2,0,1:T(2,128)(2,1)S(1)}, u32[]{:S(2)}, u32[]{:S(2)}) collective-permute-start(bf16[2,96,1536]{2,0,1:T(2,128)(2,1)S(1)} %collective-permute-done.3), channel_id=1, source_target_pairs={{2,0},{3,1},{0,2},{1,3},{6,4},{7,5},{4,6},{5,7},{10,8},{11,9},{8,1... | collective-permute-start | bytes 1769480 | tf_op jit(solution)/shard_map/ppermute | solution.py:14
  163.1 92.1 %copy-start.2 = (f32[2]{0:T(128)S(1)}, f32[2]{0:T(128)}, u32[]{:S(2)}) copy-start(f32[2]{0:T(128)} %param.9) | copy-start | bytes 28
  164.3 21.1 %collective-permute-start.5 = (bf16[2,1536,128]{2,1,0:T(8,128)(2,1)S(1)}, bf16[2,1536,128]{2,1,0:T(8,128)(2,1)S(1)}, u32[]{:S(2)}, u32[]{:S(2)}) collective-permute-start(bf16[2,1536,128]{2,1,0:T(8,128)(2,1)S(1)} %slice.100), channel_id=1, source_target_pairs={{12,0},{0,4},{4,8},{8,12},{13,1},{1,5},{5,9},{9,13},{14,2},{2,6},{... | collective-permute-start | bytes 2359304 | tf_op jit(solution)/shard_map/ppermute | solution.py:14
  185.4 9.5 %collective-permute-start.6 = (bf16[2,1536,128]{2,1,0:T(8,128)(2,1)S(1)}, bf16[2,1536,128]{2,1,0:T(8,128)(2,1)S(1)}, u32[]{:S(2)}, u32[]{:S(2)}) collective-permute-start(bf16[2,1536,128]{2,1,0:T(8,128)(2,1)S(1)} %collective-permute-done.5), channel_id=1, source_target_pairs={{1,0},{2,1},{3,2},{0,3},{5,4},{6,5},{7,6},{4,7},{9,8},{10,9},{11,1... | collective-permute-start | bytes 2359304 | tf_op jit(solution)/shard_map/ppermute | solution.py:14
  198.0 36.1 %collective-permute-start.7 = (bf16[2,1536,128]{2,1,0:T(8,128)(2,1)S(1)}, bf16[2,1536,128]{2,1,0:T(8,128)(2,1)S(1)}, u32[]{:S(2)}, u32[]{:S(2)}) collective-permute-start(bf16[2,1536,128]{2,1,0:T(8,128)(2,1)S(1)} %get-tuple-element.171), channel_id=1, source_target_pairs={{8,0},{12,4},{0,8},{4,12},{9,1},{13,5},{1,9},{5,13},{10,2},{14,6},... | collective-permute-start | bytes 2359304 | tf_op jit(solution)/shard_map/ppermute | solution.py:14
  234.1 19.6 %collective-permute-start.8 = (bf16[2,1536,128]{2,1,0:T(8,128)(2,1)S(1)}, bf16[2,1536,128]{2,1,0:T(8,128)(2,1)S(1)}, u32[]{:S(2)}, u32[]{:S(2)}) collective-permute-start(bf16[2,1536,128]{2,1,0:T(8,128)(2,1)S(1)} %collective-permute-done.7), channel_id=1, source_target_pairs={{2,0},{3,1},{0,2},{1,3},{6,4},{7,5},{4,6},{5,7},{10,8},{11,9},{8,1... | collective-permute-start | bytes 2359304 | tf_op jit(solution)/shard_map/ppermute | solution.py:14
  318.4 8.5 %copy-start = (bf16[2,1536,1536]{2,1,0:T(8,128)(2,1)S(1)}, bf16[2,1536,1536]{2,1,0:T(8,128)(2,1)}, u32[]{:S(2)}) copy-start(bf16[2,1536,1536]{2,1,0:T(8,128)(2,1)} %get-tuple-element.246) | copy-start | bytes 28311556 | tf_op jit(solution)/shard_map/while
  332.4 19.9 %collective-permute-start = (f32[2,1536,128]{1,2,0:T(8,128)S(1)}, f32[2,1536,128]{1,2,0:T(8,128)S(1)}, u32[]{:S(2)}, u32[]{:S(2)}) collective-permute-start(f32[2,1536,128]{1,2,0:T(8,128)S(1)} %maximum_add_fusion.3), channel_id=1, source_target_pairs={{3,0},{0,1},{1,2},{2,3},{7,4},{4,5},{5,6},{6,7},{11,8},{8,9},{9,10... | collective-permute-start | bytes 4718600 | tf_op jit(solution)/shard_map/while/body/eval_jaxpr/ppermute | solution.py:14
  352.3 8.5 %copy-start = (bf16[2,1536,1536]{2,1,0:T(8,128)(2,1)S(1)}, bf16[2,1536,1536]{2,1,0:T(8,128)(2,1)}, u32[]{:S(2)}) copy-start(bf16[2,1536,1536]{2,1,0:T(8,128)(2,1)} %get-tuple-element.246) | copy-start | bytes 28311556 | tf_op jit(solution)/shard_map/while
  366.3 19.9 %collective-permute-start = (f32[2,1536,128]{1,2,0:T(8,128)S(1)}, f32[2,1536,128]{1,2,0:T(8,128)S(1)}, u32[]{:S(2)}, u32[]{:S(2)}) collective-permute-start(f32[2,1536,128]{1,2,0:T(8,128)S(1)} %maximum_add_fusion.3), channel_id=1, source_target_pairs={{3,0},{0,1},{1,2},{2,3},{7,4},{4,5},{5,6},{6,7},{11,8},{8,9},{9,10... | collective-permute-start | bytes 4718600 | tf_op jit(solution)/shard_map/while/body/eval_jaxpr/ppermute | solution.py:14
  386.2 8.5 %copy-start = (bf16[2,1536,1536]{2,1,0:T(8,128)(2,1)S(1)}, bf16[2,1536,1536]{2,1,0:T(8,128)(2,1)}, u32[]{:S(2)}) copy-start(bf16[2,1536,1536]{2,1,0:T(8,128)(2,1)} %get-tuple-element.246) | copy-start | bytes 28311556 | tf_op jit(solution)/shard_map/while
  400.3 19.9 %collective-permute-start = (f32[2,1536,128]{1,2,0:T(8,128)S(1)}, f32[2,1536,128]{1,2,0:T(8,128)S(1)}, u32[]{:S(2)}, u32[]{:S(2)}) collective-permute-start(f32[2,1536,128]{1,2,0:T(8,128)S(1)} %maximum_add_fusion.3), channel_id=1, source_target_pairs={{3,0},{0,1},{1,2},{2,3},{7,4},{4,5},{5,6},{6,7},{11,8},{8,9},{9,10... | collective-permute-start | bytes 4718600 | tf_op jit(solution)/shard_map/while/body/eval_jaxpr/ppermute | solution.py:14
  420.6 10.5 %slice-start = ((s8[9437184]{0:T(1024)(128)(4,1)}), s8[4194304]{0:T(1024)(128)(4,1)S(1)}, s32[]{:S(2)}) async-start(s8[9437184]{0:T(1024)(128)(4,1)} %bitcast.106), calls=%async_computation.1 | async-start | bytes 8388608
  420.6 10.5 %slice-start.1 = ((s8[9437184]{0:T(1024)(128)(4,1)}), s8[4194304]{0:T(1024)(128)(4,1)S(1)}, s32[]{:S(2)}) async-start(s8[9437184]{0:T(1024)(128)(4,1)} %bitcast.106), calls=%async_computation.2 | async-start | bytes 8388608
  425.9 5.3 %slice-start.2 = ((s8[9437184]{0:T(1024)(128)(4,1)}), s8[1048576]{0:T(1024)(128)(4,1)S(1)}, s32[]{:S(2)}) async-start(s8[9437184]{0:T(1024)(128)(4,1)} %bitcast.106), calls=%async_computation.3 | async-start | bytes 2097152
  436.0 1.4 copy-start.1
Sparse Core Ops, SparseCore 0:
  255.3 62.7 all-gather.1
where the time goes:
time: 449 us; the launch traced here: 447 us
  waiting for transfers between devices  238 us (53%)
  local copies, waits for them, and re-layouts  74.4 us (17%)
  other arithmetic  58 us (13%)
  matrix products  56.7 us (13%)
  between operations  13.6 us (3%)
  starting transfers between devices  6.5 us (1%)
    ppermute x11, waiting for transfers between devices, from_behind(): return lax.ppermute(block, axis, route)  195 us
    dot_general x16, matrix products, matmul(): return jnp.dot(first, second, preferred_element_type=jnp.float32)  56.7 us
    all_gather x1, waiting for transfers between devices, local(): gathered = lax.all_gather(swapped, 'row', axis=2, tiled=True)  42.8 us
    select_n x1, other arithmetic, local(): direct = jnp.where(dead_row[None, :, None], zero_bf, direct)  42 us
    unnamed x11, local copies, waits for them, and re-layouts  25.3 us
    scatter x2, local copies, waits for them, and re-layouts, local(): filled = direct.at[:, miss_row, :].set(patched)  20.5 us
    slice x1, local copies, waits for them, and re-layouts, complex_product(): left_tile[0]  19.5 us
  transfers between devices with their start and end apart: 12, of which 11 were waited for; matrix products, arithmetic and copies ran while one was open for 14% of the time, Pallas kernels for 0%

commit v1 on v0

--- a/solution.py
+++ b/solution.py
@@ -82,7 +82,23 @@
     win_width = window.shape[2]
     running = jnp.zeros((2, tile_size, win_width), jnp.float32)
     swapped = transpose_blocks(window, grid_size, row_index, col_index)
-    gathered = lax.all_gather(swapped, "row", axis=2, tiled=True)
+    size, here, rows = (lax.axis_size("row"), lax.axis_index("row"), swapped.shape[2])
+    forward = [(i_2, (i_2 + 1) % size) for i_2 in range(size)]
+    downward = [(i_2, (i_2 - 1) % size) for i_2 in range(size)]
+    gathered = jnp.zeros((*swapped.shape[:2], size * rows, *swapped.shape[2 + 1 :]), swapped.dtype)
+    gathered = lax.dynamic_update_slice_in_dim(gathered, swapped, here * rows, axis=2)
+    from_left = from_right = swapped
+    half = size // 2
+    for step in range(1, half + 1):
+        from_left = lax.ppermute(from_left, "row", forward)
+        gathered = lax.dynamic_update_slice_in_dim(
+            gathered, from_left, (here - step) % size * rows, axis=2
+        )
+        if step < size - half:
+            from_right = lax.ppermute(from_right, "row", downward)
+            gathered = lax.dynamic_update_slice_in_dim(
+                gathered, from_right, (here + step) % size * rows, axis=2
+            )
 
     def one_hop(stop_index, total):
         source_block = (col_index - stop_index - 1) % grid_size

time: 449 us -> 431 us (0.960)
  waiting for transfers between devices: 238 us -> 223 us
  between operations: 13.6 us -> 0.22 us
  local copies, waits for them, and re-layouts: 74.4 us -> 79.4 us
    all_gather x1 -> x0, waiting for transfers between devices: 42.8 us -> none  [local(): gathered = lax.all_gather(swapped, 'row', axis=2, tiled=True)]
    ppermute x0 -> x3, waiting for transfers between devices: none -> 28.3 us  [the longest x2 28.3 us: local(): from_left = lax.ppermute(from_left, 'row', forward)]
  transfers between devices with their start and end apart: 12 -> 14, of which waited for: 11 -> 12; matrix products, arithmetic and copies ran while one was open for 14% -> 15% of each run, Pallas kernels for 0% -> 0%
where the time goes in v1:
time: 431 us; the launch traced here: 428 us
  waiting for transfers between devices  223 us (52%)
  local copies, waits for them, and re-layouts  79.4 us (18%)
  other arithmetic  57.8 us (13%)
  matrix products  56.7 us (13%)
  starting transfers between devices  10.3 us (2%)
    ppermute x11, waiting for transfers between devices, from_behind(): return lax.ppermute(block, axis, route)  195 us
    dot_general x16, matrix products, matmul(): return jnp.dot(first, second, preferred_element_type=jnp.float32)  56.7 us
    select_n x1, other arithmetic, local(): direct = jnp.where(dead_row[None, :, None], zero_bf, direct)  41.9 us
    ppermute x2, waiting for transfers between devices, local(): from_left = lax.ppermute(from_left, 'row', forward)  28.3 us
    unnamed x11, local copies, waits for them, and re-layouts  25.3 us
    scatter x2, local copies, waits for them, and re-layouts, local(): filled = direct.at[:, miss_row, :].set(patched)  20.5 us
    slice x1, local copies, waits for them, and re-layouts, complex_product(): left_tile[0]  19.6 us
  transfers between devices with their start and end apart: 14, of which 12 were waited for; matrix products, arithmetic and copies ran while one was open for 15% of the time, Pallas kernels for 0%

profile of v1, /device:TPU:0, one launch (start us, length us, event | category | flops | bytes accessed | tf_op | source)
XLA Modules:
  0.0 427.7 jit_solution(6678425155860232537)
XLA Ops:
  3.7 24.1 %copy.16 = bf16[2,1536,1536]{1,0,2:T(2,128)(2,1)} copy(bf16[2,1536,1536]{2,1,0:T(8,128)(2,1)} %param.6) | data formatting | bytes 18874368 | tf_op args[0]
  27.8 5.5 %gather_fusion.1 = bf16[96,2,1536]{2,1,0:T(2,128)(2,1)S(1)} fusion(bf16[2,1536,1536]{1,0,2:T(2,128)(2,1)} %copy.16, s32[1024]{0:T(1024)S(1)} %get-tuple-element.185), kind=kCustom, calls=%fused_computation.1 | custom fusion | bytes 1180032 | tf_op jit(solution)/shard_map/jit(_take)/gather | solution.py:74
  37.0 15.3 %collective-permute-done.1 = bf16[2,96,1536]{2,0,1:T(2,128)(2,1)S(1)} collective-permute-done((bf16[2,96,1536]{2,0,1:T(2,128)(2,1)S(1)}, bf16[2,96,1536]{2,0,1:T(2,128)(2,1)S(1)}, u32[]{:S(2)}, u32[]{:S(2)}) %collective-permute-start.1) | collective-permute-done | bytes 589856 | tf_op jit(solution)/shard_map/ppermute | solution.py:14
  53.1 6.8 %collective-permute-done.2 = bf16[2,96,1536]{2,0,1:T(2,128)(2,1)S(1)} collective-permute-done((bf16[2,96,1536]{2,0,1:T(2,128)(2,1)S(1)}, bf16[2,96,1536]{2,0,1:T(2,128)(2,1)S(1)}, u32[]{:S(2)}, u32[]{:S(2)}) %collective-permute-start.2) | collective-permute-done | bytes 589856 | tf_op jit(solution)/shard_map/ppermute | solution.py:14
  62.2 27.9 %collective-permute-done.3 = bf16[2,96,1536]{2,0,1:T(2,128)(2,1)S(1)} collective-permute-done((bf16[2,96,1536]{2,0,1:T(2,128)(2,1)S(1)}, bf16[2,96,1536]{2,0,1:T(2,128)(2,1)S(1)}, u32[]{:S(2)}, u32[]{:S(2)}) %collective-permute-start.3) | collective-permute-done | bytes 589856 | tf_op jit(solution)/shard_map/ppermute | solution.py:14
  91.4 41.9 %broadcast_select_fusion = bf16[2,1536,1536]{2,0,1:T(2,128)(2,1)} fusion(pred[1536]{0:T(1024)(128)(4,1)S(1)} %fusion.54, pred[1536]{0:T(1024)(128)(4,1)S(1)} %get-tuple-element.177, bf16[2,1536,1536]{2,1,0:T(8,128)(2,1)} %param.6), kind=kLoop, calls=%fused_computation.26 | loop fusion | flops 9437184 | bytes 18877440 | tf_op jit(solution)/shard_map/jit(_where)/select_n | solution.py:77
  136.1 11.7 %scatter_fusion = bf16[2,1536,1536]{2,0,1:T(2,128)(2,1)} fusion(bf16[2,1536,1536]{2,0,1:T(2,128)(2,1)} %broadcast_select_fusion, s32[96]{0:T(128)S(1)} %get-tuple-element.180, bf16[96,2,1536]{2,1,0:T(2,128)(2,1)S(1)} %fusion.52), kind=kCustom, calls=%fused_computation.2 | custom fusion | bytes 1769856 | tf_op jit(solution)/shard_map/scatter | solution.py:80
  147.7 8.8 %copy.17 = bf16[2,1536,1536]{2,1,0:T(8,128)(2,1)} copy(bf16[2,1536,1536]{2,0,1:T(2,128)(2,1)} %scatter_fusion) | data formatting | bytes 18874368 | tf_op jit(solution)/shard_map/scatter | solution.py:80
  157.8 21.1 %collective-permute-done.5 = bf16[2,1536,128]{2,1,0:T(8,128)(2,1)S(1)} collective-permute-done((bf16[2,1536,128]{2,1,0:T(8,128)(2,1)S(1)}, bf16[2,1536,128]{2,1,0:T(8,128)(2,1)S(1)}, u32[]{:S(2)}, u32[]{:S(2)}) %collective-permute-start.5) | collective-permute-done | bytes 786464 | tf_op jit(solution)/shard_map/ppermute | solution.py:14
  178.9 9.5 %collective-permute-done.6 = bf16[2,1536,128]{2,1,0:T(8,128)(2,1)S(1)} collective-permute-done((bf16[2,1536,128]{2,1,0:T(8,128)(2,1)S(1)}, bf16[2,1536,128]{2,1,0:T(8,128)(2,1)S(1)}, u32[]{:S(2)}, u32[]{:S(2)}) %collective-permute-start.6) | collective-permute-done | bytes 786464 | tf_op jit(solution)/shard_map/ppermute | solution.py:14
  191.4 36.1 %collective-permute-done.7 = bf16[2,1536,128]{2,1,0:T(8,128)(2,1)S(1)} collective-permute-done((bf16[2,1536,128]{2,1,0:T(8,128)(2,1)S(1)}, bf16[2,1536,128]{2,1,0:T(8,128)(2,1)S(1)}, u32[]{:S(2)}, u32[]{:S(2)}) %collective-permute-start.7) | collective-permute-done | bytes 786464 | tf_op jit(solution)/shard_map/ppermute | solution.py:14
  228.3 18.7 %collective-permute-done.8 = bf16[2,1536,128]{2,1,0:T(8,128)(2,1)S(1)} collective-permute-done((bf16[2,1536,128]{2,1,0:T(8,128)(2,1)S(1)}, bf16[2,1536,128]{2,1,0:T(8,128)(2,1)S(1)}, u32[]{:S(2)}, u32[]{:S(2)}) %collective-permute-start.8) | collective-permute-done | bytes 786464 | tf_op jit(solution)/shard_map/ppermute | solution.py:14
  254.9 17.8 %collective-permute-done.9 = bf16[2,1536,128]{2,1,0:T(8,128)(2,1)S(1)} collective-permute-done((bf16[2,1536,128]{2,1,0:T(8,128)(2,1)S(1)}, bf16[2,1536,128]{2,1,0:T(8,128)(2,1)S(1)}, u32[]{:S(2)}, u32[]{:S(2)}) %collective-permute-start.9) | collective-permute-done | bytes 786464 | tf_op jit(solution)/shard_map/ppermute | solution.py:93
  272.7 19.6 %fusion.69 = (bf16[1,1536,1536]{2,0,1:T(2,128)(2,1)}, bf16[1,1536,1536]{2,0,1:T(2,128)(2,1)}) fusion(bf16[2,1536,1536]{2,0,1:T(2,128)(2,1)} %scatter_fusion), kind=kLoop, calls=%fused_computation.108 | loop fusion | bytes 18874368 | tf_op jit(solution)/shard_map/slice | solution.py:22
  294.3 10.4 %collective-permute-done.11 = bf16[2,1536,128]{2,1,0:T(8,128)(2,1)S(1)} collective-permute-done((bf16[2,1536,128]{2,1,0:T(8,128)(2,1)S(1)}, bf16[2,1536,128]{2,1,0:T(8,128)(2,1)S(1)}, u32[]{:S(2)}, u32[]{:S(2)}) %collective-permute-start.11) | collective-permute-done | bytes 786464 | tf_op jit(solution)/shard_map/ppermute | solution.py:93
  305.9 101.8 %while.15 = (s32[]{:T(128)}, f32[2,1536,128]{1,2,0:T(8,128)S(1)}, s32[]{:T(128)}, bf16[2,1536,512]{2,1,0:T(8,128)(2,1)}, bf16[2,1536,1536]{2,1,0:T(8,128)(2,1)},...) while((s32[]{:T(128)}, f32[2,1536,128]{1,2,0:T(8,128)S(1)}, ...), condition=%wide.region_6.7_spmd, body=%wide.region_5.6_spmd.sunk | while | flops 2417098752 | bytes 73925016 | solution.py:109
  306.0 4.3 %fusion.83 = f32[128,1536]{1,0:T(8,128)S(1)} fusion(bf16[2,1536,1536]{2,1,0:T(8,128)(2,1)} %get-tuple-element.248, bf16[2,1536,512]{2,1,0:T(8,128)(2,1)} %get-tuple-element.247, s32[]{:T(128)S(6)} %select_n.330), kind=kOutput, calls=%fused_computation.3.clone.1 | convolution fusion | flops 603979776 | bytes 5898244 | tf_op jit(solution)/shard_map/while/body/eval_jaxpr/dot_general | solution.py:18
  320.1 19.8 %collective-permute-done = f32[2,1536,128]{1,2,0:T(8,128)S(1)} collective-permute-done((f32[2,1536,128]{1,2,0:T(8,128)S(1)}, f32[2,1536,128]{1,2,0:T(8,128)S(1)}, u32[]{:S(2)}, u32[]{:S(2)}) %collective-permute-start) | collective-permute-done | bytes 1572896 | tf_op jit(solution)/shard_map/while/body/eval_jaxpr/ppermute | solution.py:14
  339.9 4.3 %fusion.83 = f32[128,1536]{1,0:T(8,128)S(1)} fusion(bf16[2,1536,1536]{2,1,0:T(8,128)(2,1)} %get-tuple-element.248, bf16[2,1536,512]{2,1,0:T(8,128)(2,1)} %get-tuple-element.247, s32[]{:T(128)S(6)} %select_n.330), kind=kOutput, calls=%fused_computation.3.clone.1 | convolution fusion | flops 603979776 | bytes 5898244 | tf_op jit(solution)/shard_map/while/body/eval_jaxpr/dot_general | solution.py:18
  354.0 19.8 %collective-permute-done = f32[2,1536,128]{1,2,0:T(8,128)S(1)} collective-permute-done((f32[2,1536,128]{1,2,0:T(8,128)S(1)}, f32[2,1536,128]{1,2,0:T(8,128)S(1)}, u32[]{:S(2)}, u32[]{:S(2)}) %collective-permute-start) | collective-permute-done | bytes 1572896 | tf_op jit(solution)/shard_map/while/body/eval_jaxpr/ppermute | solution.py:14
  373.8 4.3 %fusion.83 = f32[128,1536]{1,0:T(8,128)S(1)} fusion(bf16[2,1536,1536]{2,1,0:T(8,128)(2,1)} %get-tuple-element.248, bf16[2,1536,512]{2,1,0:T(8,128)(2,1)} %get-tuple-element.247, s32[]{:T(128)S(6)} %select_n.330), kind=kOutput, calls=%fused_computation.3.clone.1 | convolution fusion | flops 603979776 | bytes 5898244 | tf_op jit(solution)/shard_map/while/body/eval_jaxpr/dot_general | solution.py:18
  387.9 19.8 %collective-permute-done = f32[2,1536,128]{1,2,0:T(8,128)S(1)} collective-permute-done((f32[2,1536,128]{1,2,0:T(8,128)S(1)}, f32[2,1536,128]{1,2,0:T(8,128)S(1)}, u32[]{:S(2)}, u32[]{:S(2)}) %collective-permute-start) | collective-permute-done | bytes 1572896 | tf_op jit(solution)/shard_map/while/body/eval_jaxpr/ppermute | solution.py:14
  408.2 5.3 %fusion.28 = f32[1536,128]{1,0:T(8,128)S(1)} fusion(bf16[1,1536,1536]{2,0,1:T(2,128)(2,1)} %get-tuple-element.172, bf16[2,1536,512]{2,1,0:T(8,128)(2,1)} %constant_dynamic-update-slice_fusion, s32[]{:T(128)S(6)} %select_n.256), kind=kOutput, calls=%fused_computation.28 | convolution fusion | flops 603979776 | bytes 10616836 | tf_op jit(solution)/shard_map/dot_general | solution.py:18
  413.5 5.2 %fusion.30 = f32[1536,128]{1,0:T(8,128)S(1)} fusion(bf16[1,1536,1536]{2,0,1:T(2,128)(2,1)} %get-tuple-element.172, bf16[2,1536,512]{2,1,0:T(8,128)(2,1)} %constant_dynamic-update-slice_fusion, s32[]{:T(128)S(6)} %add.255, s32[]{:T(128)S(6)} %select_n.256), kind=kOutput, calls=%fused_computation.30 | convolution fusion | flops 603979776 | bytes 10616840 | tf_op jit(solution)/shard_map/dot_general | solution.py:18
  (74 shorter events, 69.2 us)
Async XLA Ops:
  33.9 18.4 %collective-permute-start.1 = (bf16[2,96,1536]{2,0,1:T(2,128)(2,1)S(1)}, bf16[2,96,1536]{2,0,1:T(2,128)(2,1)S(1)}, u32[]{:S(2)}, u32[]{:S(2)}) collective-permute-start(bf16[2,96,1536]{2,0,1:T(2,128)(2,1)S(1)} %fusion.53), channel_id=1, source_target_pairs={{12,0},{0,4},{4,8},{8,12},{13,1},{1,5},{5,9},{9,13},{14,2},{2,6},{... | collective-permute-start | bytes 1769480 | tf_op jit(solution)/shard_map/ppermute | solution.py:14
  52.3 7.6 %collective-permute-start.2 = (bf16[2,96,1536]{2,0,1:T(2,128)(2,1)S(1)}, bf16[2,96,1536]{2,0,1:T(2,128)(2,1)S(1)}, u32[]{:S(2)}, u32[]{:S(2)}) collective-permute-start(bf16[2,96,1536]{2,0,1:T(2,128)(2,1)S(1)} %collective-permute-done.1), channel_id=1, source_target_pairs={{1,0},{2,1},{3,2},{0,3},{5,4},{6,5},{7,6},{4,7},{9,8},{10,9},{11,1... | collective-permute-start | bytes 1769480 | tf_op jit(solution)/shard_map/ppermute | solution.py:14
  61.3 28.7 %collective-permute-start.3 = (bf16[2,96,1536]{2,0,1:T(2,128)(2,1)S(1)}, bf16[2,96,1536]{2,0,1:T(2,128)(2,1)S(1)}, u32[]{:S(2)}, u32[]{:S(2)}) collective-permute-start(bf16[2,96,1536]{2,0,1:T(2,128)(2,1)S(1)} %broadcast_select_fusion.3), channel_id=1, source_target_pairs={{8,0},{12,4},{0,8},{4,12},{9,1},{13,5},{1,9},{5,13},{10,2},{14,6},... | collective-permute-start | bytes 1769480 | tf_op jit(solution)/shard_map/ppermute | solution.py:14
  90.0 44.3 %collective-permute-start.4 = (bf16[2,96,1536]{2,0,1:T(2,128)(2,1)S(1)}, bf16[2,96,1536]{2,0,1:T(2,128)(2,1)S(1)}, u32[]{:S(2)}, u32[]{:S(2)}) collective-permute-start(bf16[2,96,1536]{2,0,1:T(2,128)(2,1)S(1)} %collective-permute-done.3), channel_id=1, source_target_pairs={{2,0},{3,1},{0,2},{1,3},{6,4},{7,5},{4,6},{5,7},{10,8},{11,9},{8,1... | collective-permute-start | bytes 1769480 | tf_op jit(solution)/shard_map/ppermute | solution.py:14
  157.7 21.1 %collective-permute-start.5 = (bf16[2,1536,128]{2,1,0:T(8,128)(2,1)S(1)}, bf16[2,1536,128]{2,1,0:T(8,128)(2,1)S(1)}, u32[]{:S(2)}, u32[]{:S(2)}) collective-permute-start(bf16[2,1536,128]{2,1,0:T(8,128)(2,1)S(1)} %slice.100), channel_id=1, source_target_pairs={{12,0},{0,4},{4,8},{8,12},{13,1},{1,5},{5,9},{9,13},{14,2},{2,6},{... | collective-permute-start | bytes 2359304 | tf_op jit(solution)/shard_map/ppermute | solution.py:14
  178.9 9.5 %collective-permute-start.6 = (bf16[2,1536,128]{2,1,0:T(8,128)(2,1)S(1)}, bf16[2,1536,128]{2,1,0:T(8,128)(2,1)S(1)}, u32[]{:S(2)}, u32[]{:S(2)}) collective-permute-start(bf16[2,1536,128]{2,1,0:T(8,128)(2,1)S(1)} %collective-permute-done.5), channel_id=1, source_target_pairs={{1,0},{2,1},{3,2},{0,3},{5,4},{6,5},{7,6},{4,7},{9,8},{10,9},{11,1... | collective-permute-start | bytes 2359304 | tf_op jit(solution)/shard_map/ppermute | solution.py:14
  191.4 36.1 %collective-permute-start.7 = (bf16[2,1536,128]{2,1,0:T(8,128)(2,1)S(1)}, bf16[2,1536,128]{2,1,0:T(8,128)(2,1)S(1)}, u32[]{:S(2)}, u32[]{:S(2)}) collective-permute-start(bf16[2,1536,128]{2,1,0:T(8,128)(2,1)S(1)} %get-tuple-element.173), channel_id=1, source_target_pairs={{8,0},{12,4},{0,8},{4,12},{9,1},{13,5},{1,9},{5,13},{10,2},{14,6},... | collective-permute-start | bytes 2359304 | tf_op jit(solution)/shard_map/ppermute | solution.py:14
  227.5 19.6 %collective-permute-start.8 = (bf16[2,1536,128]{2,1,0:T(8,128)(2,1)S(1)}, bf16[2,1536,128]{2,1,0:T(8,128)(2,1)S(1)}, u32[]{:S(2)}, u32[]{:S(2)}) collective-permute-start(bf16[2,1536,128]{2,1,0:T(8,128)(2,1)S(1)} %collective-permute-done.7), channel_id=1, source_target_pairs={{2,0},{3,1},{0,2},{1,3},{6,4},{7,5},{4,6},{5,7},{10,8},{11,9},{8,1... | collective-permute-start | bytes 2359304 | tf_op jit(solution)/shard_map/ppermute | solution.py:14
  228.3 22.2 %copy-start.2 = (f32[2]{0:T(128)S(1)}, f32[2]{0:T(128)}, u32[]{:S(2)}) copy-start(f32[2]{0:T(128)} %param.9) | copy-start | bytes 28
  250.5 22.2 %collective-permute-start.9 = (bf16[2,1536,128]{2,1,0:T(8,128)(2,1)S(1)}, bf16[2,1536,128]{2,1,0:T(8,128)(2,1)S(1)}, u32[]{:S(2)}, u32[]{:S(2)}) collective-permute-start(bf16[2,1536,128]{2,1,0:T(8,128)(2,1)S(1)} %get-tuple-element.166), channel_id=1, source_target_pairs={{0,4},{4,8},{8,12},{12,0},{1,5},{5,9},{9,13},{13,1},{2,6},{6,10},{... | collective-permute-start | bytes 2359304 | tf_op jit(solution)/shard_map/ppermute | solution.py:93
  251.1 42.3 %collective-permute-start.10 = (bf16[2,1536,128]{2,1,0:T(8,128)(2,1)S(1)}, bf16[2,1536,128]{2,1,0:T(8,128)(2,1)S(1)}, u32[]{:S(2)}, u32[]{:S(2)}) collective-permute-start(bf16[2,1536,128]{2,1,0:T(8,128)(2,1)S(1)} %get-tuple-element.166), channel_id=1, source_target_pairs={{0,12},{4,0},{8,4},{12,8},{1,13},{5,1},{9,5},{13,9},{2,14},{6,2},{... | collective-permute-start | bytes 2359304 | tf_op jit(solution)/shard_map/ppermute | solution.py:98
  272.7 32.0 %collective-permute-start.11 = (bf16[2,1536,128]{2,1,0:T(8,128)(2,1)S(1)}, bf16[2,1536,128]{2,1,0:T(8,128)(2,1)S(1)}, u32[]{:S(2)}, u32[]{:S(2)}) collective-permute-start(bf16[2,1536,128]{2,1,0:T(8,128)(2,1)S(1)} %collective-permute-done.9), channel_id=1, source_target_pairs={{0,4},{4,8},{8,12},{12,0},{1,5},{5,9},{9,13},{13,1},{2,6},{6,10},{... | collective-permute-start | bytes 2359304 | tf_op jit(solution)/shard_map/ppermute | solution.py:93
  306.0 8.5 %copy-start = (bf16[2,1536,1536]{2,1,0:T(8,128)(2,1)S(1)}, bf16[2,1536,1536]{2,1,0:T(8,128)(2,1)}, u32[]{:S(2)}) copy-start(bf16[2,1536,1536]{2,1,0:T(8,128)(2,1)} %get-tuple-element.248) | copy-start | bytes 28311556 | tf_op jit(solution)/shard_map/while
  320.0 19.9 %collective-permute-start = (f32[2,1536,128]{1,2,0:T(8,128)S(1)}, f32[2,1536,128]{1,2,0:T(8,128)S(1)}, u32[]{:S(2)}, u32[]{:S(2)}) collective-permute-start(f32[2,1536,128]{1,2,0:T(8,128)S(1)} %maximum_add_fusion.3), channel_id=1, source_target_pairs={{3,0},{0,1},{1,2},{2,3},{7,4},{4,5},{5,6},{6,7},{11,8},{8,9},{9,10... | collective-permute-start | bytes 4718600 | tf_op jit(solution)/shard_map/while/body/eval_jaxpr/ppermute | solution.py:14
  339.9 8.5 %copy-start = (bf16[2,1536,1536]{2,1,0:T(8,128)(2,1)S(1)}, bf16[2,1536,1536]{2,1,0:T(8,128)(2,1)}, u32[]{:S(2)}) copy-start(bf16[2,1536,1536]{2,1,0:T(8,128)(2,1)} %get-tuple-element.248) | copy-start | bytes 28311556 | tf_op jit(solution)/shard_map/while
  353.9 19.9 %collective-permute-start = (f32[2,1536,128]{1,2,0:T(8,128)S(1)}, f32[2,1536,128]{1,2,0:T(8,128)S(1)}, u32[]{:S(2)}, u32[]{:S(2)}) collective-permute-start(f32[2,1536,128]{1,2,0:T(8,128)S(1)} %maximum_add_fusion.3), channel_id=1, source_target_pairs={{3,0},{0,1},{1,2},{2,3},{7,4},{4,5},{5,6},{6,7},{11,8},{8,9},{9,10... | collective-permute-start | bytes 4718600 | tf_op jit(solution)/shard_map/while/body/eval_jaxpr/ppermute | solution.py:14
  373.8 8.5 %copy-start = (bf16[2,1536,1536]{2,1,0:T(8,128)(2,1)S(1)}, bf16[2,1536,1536]{2,1,0:T(8,128)(2,1)}, u32[]{:S(2)}) copy-start(bf16[2,1536,1536]{2,1,0:T(8,128)(2,1)} %get-tuple-element.248) | copy-start | bytes 28311556 | tf_op jit(solution)/shard_map/while
  387.8 19.9 %collective-permute-start = (f32[2,1536,128]{1,2,0:T(8,128)S(1)}, f32[2,1536,128]{1,2,0:T(8,128)S(1)}, u32[]{:S(2)}, u32[]{:S(2)}) collective-permute-start(f32[2,1536,128]{1,2,0:T(8,128)S(1)} %maximum_add_fusion.3), channel_id=1, source_target_pairs={{3,0},{0,1},{1,2},{2,3},{7,4},{4,5},{5,6},{6,7},{11,8},{8,9},{9,10... | collective-permute-start | bytes 4718600 | tf_op jit(solution)/shard_map/while/body/eval_jaxpr/ppermute | solution.py:14
  408.2 10.5 %slice-start = ((s8[9437184]{0:T(1024)(128)(4,1)}), s8[4194304]{0:T(1024)(128)(4,1)S(1)}, s32[]{:S(2)}) async-start(s8[9437184]{0:T(1024)(128)(4,1)} %bitcast.106), calls=%async_computation | async-start | bytes 8388608
  408.2 10.5 %slice-start.1 = ((s8[9437184]{0:T(1024)(128)(4,1)}), s8[4194304]{0:T(1024)(128)(4,1)S(1)}, s32[]{:S(2)}) async-start(s8[9437184]{0:T(1024)(128)(4,1)} %bitcast.106), calls=%async_computation.1 | async-start | bytes 8388608
  413.5 5.3 %slice-start.2 = ((s8[9437184]{0:T(1024)(128)(4,1)}), s8[1048576]{0:T(1024)(128)(4,1)S(1)}, s32[]{:S(2)}) async-start(s8[9437184]{0:T(1024)(128)(4,1)} %bitcast.106), calls=%async_computation.2 | async-start | bytes 2097152
  423.6 1.4 copy-start.1
